TPU v7x, 32 devices: a whole 2x2x4 slice. The times are simulated.
32 devices in a mesh: gx: 4 (over z), gy: 8 (over y, x, core).
Axes of the slice: x: 2, y: 2, z: 4, core: 2. Of those that a mesh axis runs over, the one named last changes fastest.
Arguments:
- child_dens: bfloat16 [296, 8192], P(None, ('gx', 'gy')), may hold values from -0.625 to 0.625
- users: int32 [2048], P(('gx', 'gy')), may hold values from 0 to 31
- local_dens: bfloat16 [296, 16384], P(None, ('gx', 'gy')), may hold values from -6 to 6
- live: int32 [32], P(('gx', 'gy')), may hold values from 16 to 128, as said below
- m2l_ops: bfloat16 [296, 2368], replicated, may hold values from -0.125 to 0.125
- m2l_lists: int32 [8, 4096], P(None, ('gx', 'gy')), may hold values from -1 to 143, as said below
- leaf_pos: float32 [3, 131072], P(None, ('gx', 'gy')), may hold values from 0 to 1
- leaf_charge: float32 [4, 131072], P(None, ('gx', 'gy')), may hold values from -0.2 to 0.2
- leaf_nbrs: int32 [4096, 27], P(('gx', 'gy')), may hold values from -1 to 159, as said below
Outputs:
- local_exp: float32 [296, 16384], P(None, ('gx', 'gy'))
- near_pot: float32 [4, 131072], P(None, ('gx', 'gy'))
Inputs may be any that keep to these rules, and one draw needn't show every extreme that they name: `live`: at least 16 on every device; some device has exactly 128. `m2l_lists`: entry for target slot k lies in k .. k + 16 or is -1. `leaf_nbrs`: entry for leaf l of a device lies in l .. l + 32 or is -1; the first entry is the leaf itself, l + 16.
All inputs are finite; a program needn't handle non-finite values.
Results may differ from a plain program's by a relative error of at most 0.00071.
Values may be sent and summed in bfloat16 or wider, within the bound.
A program may use at most 128 MiB of HBM per device.

v0:
```python
import functools

import jax
import jax.numpy as jnp
from jax import lax
from jax.experimental import pallas as pl
from jax.experimental.pallas import tpu as pltpu
from jax.sharding import PartitionSpec as P

Q = 4
NOFF = 8
SH_DEV = 1
NPT = 32
HL = 16
GROUP = 8
BLOCK = 32

soften = 0.01
f32 = jnp.float32
bf16 = jnp.bfloat16
MESH = pl.DeviceIdType.MESH


def split3(value):
    first = value.astype(bf16).astype(f32)
    rest = value - first
    second = rest.astype(bf16).astype(f32)
    return first, second, rest - second


def row_ids(shape):
    return lax.broadcasted_iota(jnp.int32, shape, 0)


def lane_ids(shape):
    return lax.broadcasted_iota(jnp.int32, shape, 1)


def with_norm(coords):
    norm = jnp.sum(coords * coords, axis=0, keepdims=True)
    return jnp.where(row_ids(coords.shape) == 3, norm, coords), norm


def source_rows(coords):
    value, _ = with_norm(coords)
    one, two, three = split3(value)
    flat = jnp.where(row_ids(value.shape) < 3, f32(1.0), f32(0.0))
    return jnp.concatenate(
        [one, two, three, one, two, one, flat, jnp.zeros_like(one)], axis=0
    ).astype(bf16)


def target_rows(coords):
    value, norm = with_norm(coords)
    one, two, three = split3(value)
    row = row_ids(value.shape)
    main = jnp.where(row < 3, -2.0 * one, jnp.where(row == 3, f32(1.0), f32(0.0)))
    second = jnp.where(row < 3, -2.0 * two, f32(0.0))
    third = jnp.where(row < 3, -2.0 * three, f32(0.0))
    part = split3(norm + soften)
    flat = jnp.where(
        row == 0,
        part[0],
        jnp.where(row == 1, part[1], jnp.where(row == 2, part[2], f32(0.0))),
    )
    return jnp.concatenate(
        [main, main, main, second, second, third, flat, jnp.zeros_like(one)], axis=0
    ).astype(bf16)


def near_counts(nbrs, counts):
    slots, leaves = nbrs.shape
    groups, eight, reach = counts.shape
    span = GROUP + 2 * HL
    rows = -(-span // 16) * 16
    base = nbrs - lane_ids(nbrs.shape) // GROUP * GROUP
    base = jnp.where(nbrs < 0, -1, base)
    ids = row_ids((rows, leaves))
    total = jnp.zeros((rows, leaves), f32)
    for j in range(slots):
        total = total + jnp.where(ids == base[j : j + 1, :], f32(1.0), f32(0.0))
    spread = row_ids((rows, reach)) == lane_ids((rows, reach)) // NPT
    full = lax.dot_general(
        total.T.astype(bf16),
        jnp.where(spread, f32(1.0), f32(0.0)).astype(bf16),
        (((1,), (0,)), ((), ())),
        preferred_element_type=f32,
    )
    counts[...] = full.reshape(groups, eight, reach)


def near_group(g, sources, targets, charges, counts, out):
    reach = counts.shape[2]
    size = GROUP * NPT
    rows = Q * GROUP
    start = pl.multiple_of(g * size, size)
    right = targets[:, pl.ds(start, size)]
    cnt = counts[g]
    ch = charges[:, pl.ds(start, reach)]
    w = jnp.concatenate([cnt * ch[q : q + 1] for q in range(Q)], axis=0)
    wh = w.astype(bf16)
    wl = (w - wh.astype(f32)).astype(bf16)
    w = jnp.concatenate([wh, wl], axis=0)
    total = jnp.zeros((2 * rows, size), f32)
    for at in range(0, reach, 256):
        width = min(256, reach - at)
        left = sources[pl.ds(pl.multiple_of(start + at, size), width), :]
        kernel = lax.rsqrt(jnp.dot(left, right, preferred_element_type=f32))
        high = kernel.astype(bf16)
        low = (kernel - high.astype(f32)).astype(bf16)
        span = slice(at, at + width)
        total = total + jnp.dot(w[:, span], high, preferred_element_type=f32)
        total = total + jnp.dot(w[:, span], low, preferred_element_type=f32)
    flat = total[:rows] + total[rows:]
    mine = row_ids(flat.shape) % GROUP == lane_ids(flat.shape) // NPT
    flat = jnp.where(mine, flat, f32(0.0))
    out[:, pl.ds(start, size)] = jnp.sum(flat.reshape(Q, GROUP, size), axis=1)


def alive_lanes(live, slots, shape):
    slot = lane_ids(shape) // Q
    lower = live // 2
    return (slot < lower) | (slot >= slots - (live - lower))


def m2l_gather(window, lists, gathered):
    offsets, slots = lists.shape
    surface = window.shape[0]
    wide = slots * Q
    expand = row_ids((slots, wide)) == lane_ids((slots, wide)) // Q
    place = jnp.dot(
        (lists + 1).astype(f32).astype(bf16),
        jnp.where(expand, f32(1.0), f32(0.0)).astype(bf16),
        preferred_element_type=f32,
    ).astype(jnp.int32)
    place = (place - 1) * Q + lane_ids(place.shape) % Q
    size = BLOCK * Q
    depth = (BLOCK + slots // 8) * Q
    for b in range(slots // BLOCK):
        block = window[:, b * size : b * size + depth]
        ids = row_ids((depth, size)) + b * size
        for o in range(0, offsets, 2):
            hits = [
                ids == place[k : k + 1, b * size : (b + 1) * size] for k in (o, o + 1)
            ]
            hot = jnp.concatenate([jnp.where(hit, f32(1.0), f32(0.0)) for hit in hits], axis=1)
            pair = jnp.dot(block, hot.astype(bf16), preferred_element_type=f32)
            both = jnp.concatenate([pair[:, :size], pair[:, size:]], axis=0).astype(bf16)
            gathered[o * surface : (o + 2) * surface, b * size : (b + 1) * size] = both


def partial_sums(child, users, send, nx, ny):
    own = SH_DEV * Q
    rows = send.shape[0]
    chunks, count = users.shape
    wide = count * Q
    row = row_ids((rows, wide))
    owner = row // own % nx * ny + row // (own * nx)
    target = owner * own + row % own
    expand = row_ids((count, wide)) == lane_ids((count, wide)) // Q
    expand = jnp.where(expand, f32(1.0), f32(0.0)).astype(bf16)

    def chunk_sum(i):
        ids = users[pl.ds(i, 1), :]
        both = jnp.concatenate([ids // 256, ids % 256], axis=0)
        both = jnp.concatenate([both, both, both, both], axis=0)
        place = jnp.dot(
            both.astype(f32).astype(bf16), expand, preferred_element_type=f32
        ).astype(jnp.int32)
        place = (place[0:1] * 256 + place[1:2]) * Q + lane_ids((1, wide)) % Q
        hot = jnp.where(target == place, f32(1.0), f32(0.0)).astype(bf16)
        block = child[:, pl.ds(pl.multiple_of(i * wide, wide), wide)]
        return lax.dot_general(
            hot, block, (((1,), (1,)), ((), ())), preferred_element_type=f32
        )

    send[...] = chunk_sum(0)
    if chunks > 1:

        def step(i, carry):
            send[...] += chunk_sum(i)
            return carry

        lax.fori_loop(1, chunks, step, 0)


def fused_kernel(
    nx,
    ny,
    live,
    child,
    users,
    local,
    pos,
    charge,
    nbrs,
    window,
    out,
    send1,
    recv1,
    send2,
    recv2,
    spread,
    first,
    last,
    low,
    high,
    pos_low,
    pos_high,
    charge_low,
    charge_high,
    coords,
    charges,
    sources,
    targets,
    counts,
    send_sem,
    recv_sem,
):
    mx, my = lax.axis_index("gx"), lax.axis_index("gy")
    total = nx * ny
    me = mx * ny + my
    after, before = lax.rem(me + 1, total), lax.rem(me + total - 1, total)
    after = (after // ny, lax.rem(after, ny))
    before = (before // ny, lax.rem(before, ny))
    along_y = [(mx, lax.rem(my + d, ny)) for d in range(1, ny)]
    along_x = [(lax.rem(mx + d, nx), my) for d in range(1, nx)]

    barrier = pltpu.get_barrier_semaphore()
    for device in along_y + along_x + [after, before]:
        pl.semaphore_signal(barrier, inc=1, device_id=device, device_id_type=MESH)

    surface, wide = local.shape
    slots = wide // Q
    rim = low.shape[1]
    halo = pos_low.shape[1]
    count = pos.shape[1]
    own = SH_DEV * Q
    message = nx * own
    partial_sums(child, users, send1, nx, ny)
    alive = alive_lanes(live[0], slots, (surface, wide))
    owned = jnp.where(alive, local[...].astype(f32), f32(0.0)).astype(bf16)
    last[...] = owned[:, wide - rim :]
    pl.semaphore_wait(barrier, len(along_y) + len(along_x) + 2)

    at = [0]

    def remote(src, dst, device):
        k = at[0]
        at[0] += 1
        copy = pltpu.make_async_remote_copy(
            src_ref=src,
            dst_ref=dst,
            send_sem=send_sem.at[k],
            recv_sem=recv_sem.at[k],
            device_id=device,
            device_id_type=MESH,
        )
        copy.start()
        return copy

    step1 = []
    for d in range(1, ny):
        start = pl.multiple_of(lax.rem(my + d, ny) * message, message)
        step1.append(
            remote(send1.at[pl.ds(start, message), :], recv1.at[d - 1], along_y[d - 1])
        )
    leaf = [
        remote(pos.at[:, count - halo : count], pos_low, after),
        remote(charge.at[:, count - halo : count], charge_low, after),
        remote(pos.at[:, 0:halo], pos_high, before),
        remote(charge.at[:, 0:halo], charge_high, before),
    ]
    rims = [remote(last, low, after)]

    coords[...] = jnp.zeros_like(coords)
    coords[0:3, halo : halo + count] = pos[...]
    charges[:, halo : halo + count] = charge[...]
    mine = coords[:, halo : halo + count]
    sources[halo : halo + count, :] = source_rows(mine).T
    targets[...] = target_rows(mine)
    near_counts(nbrs[...], counts)
    groups = counts.shape[0]
    skip = halo // (GROUP * NPT)

    def step(g, carry):
        near_group(g, sources, targets, charges, counts, out)
        return carry

    third = (groups - 2 * skip) // 3
    lax.fori_loop(skip, skip + third, step, 0, unroll=4)

    for copy in step1:
        copy.wait()
    value = send1[pl.ds(pl.multiple_of(my * message, message), message), :]
    for d in range(ny - 1):
        value = value + recv1[d]
    for k in range(nx):
        send2[k] = value[k * own : (k + 1) * own]
    step2 = []
    for d in range(1, nx):
        step2.append(remote(send2.at[lax.rem(mx + d, nx)], recv2.at[d - 1], along_x[d - 1]))

    lax.fori_loop(skip + third, skip + 2 * third, step, 0, unroll=4)

    for copy in step2:
        copy.wait()
    shared = send2[mx]
    for d in range(nx - 1):
        shared = shared + recv2[d]
    spread[...] = jnp.zeros_like(spread)
    spread[0:own, :] = shared
    lanes = spread.shape[0]
    front = local[:, 0:lanes].astype(f32) + spread[...].T
    front = jnp.where(alive[:, 0:lanes], front, f32(0.0)).astype(bf16)
    first[...] = front[:, 0:rim]
    rims.append(remote(first, high, before))
    window[:, rim : rim + lanes] = front
    window[:, rim + lanes : rim + wide] = owned[:, lanes:]

    lax.fori_loop(skip + 2 * third, groups - skip, step, 0, unroll=4)

    for copy in leaf:
        copy.wait()
    has_low = me > 0
    has_high = me < total - 1
    for pos_ref, charge_ref, start, there in (
        (pos_low, charge_low, 0, has_low),
        (pos_high, charge_high, halo + count, has_high),
    ):
        span = slice(start, start + halo)
        coords[0:3, span] = pos_ref[...]
        charges[:, span] = jnp.where(there, charge_ref[...], f32(0.0))
        sources[span, :] = source_rows(coords[:, span]).T
    lax.fori_loop(0, skip, step, 0, unroll=2)
    lax.fori_loop(groups - skip, groups, step, 0, unroll=2)

    for copy in rims:
        copy.wait()
    window[:, 0:rim] = jnp.where(has_low, low[...], jnp.zeros_like(low))
    window[:, rim + wide :] = jnp.where(has_high, high[...], jnp.zeros_like(high))


def fused(live, child, users, local, pos, charge, nbrs):
    nx, ny = lax.axis_size("gx"), lax.axis_size("gy")
    surface, wide = local.shape
    count = pos.shape[1]
    halo = HL * NPT
    groups = count // NPT // GROUP
    span = count + 2 * halo
    reach = (GROUP + 2 * HL) * NPT
    rim = wide // 16
    own = SH_DEV * Q
    copies = ny - 1 + nx - 1 + 6
    vmem = pl.BlockSpec(memory_space=pltpu.VMEM)
    return pl.pallas_call(
        functools.partial(fused_kernel, nx, ny),
        out_shape=(
            jax.ShapeDtypeStruct((surface, wide + 2 * rim), bf16),
            jax.ShapeDtypeStruct(charge.shape, f32),
        ),
        in_specs=[pl.BlockSpec(memory_space=pltpu.SMEM)] + [vmem] * 6,
        out_specs=(vmem, vmem),
        scratch_shapes=[
            pltpu.VMEM((ny * nx * own, surface), f32),
            pltpu.VMEM((ny - 1, nx * own, surface), f32),
            pltpu.VMEM((nx, own, surface), f32),
            pltpu.VMEM((nx - 1, own, surface), f32),
            pltpu.VMEM((128, surface), f32),
            pltpu.VMEM((surface, rim), bf16),
            pltpu.VMEM((surface, rim), bf16),
            pltpu.VMEM((surface, rim), bf16),
            pltpu.VMEM((surface, rim), bf16),
            pltpu.VMEM((3, halo), f32),
            pltpu.VMEM((3, halo), f32),
            pltpu.VMEM((Q, halo), f32),
            pltpu.VMEM((Q, halo), f32),
            pltpu.VMEM((8, span), f32),
            pltpu.VMEM((Q, span), f32),
            pltpu.VMEM((span, 64), bf16),
            pltpu.VMEM((64, count), bf16),
            pltpu.VMEM((groups, GROUP, reach), f32),
            pltpu.SemaphoreType.DMA((copies,)),
            pltpu.SemaphoreType.DMA((copies,)),
        ],
        compiler_params=pltpu.CompilerParams(collective_id=0, has_side_effects=True),
    )(live, child, users.reshape(-1, 64), local, pos, charge, nbrs.T)


def m2l_kernel(live, window, lists, ops, near, out, near_out, gathered, held, sem):
    fetch = pltpu.make_async_copy(ops, held, sem)
    fetch.start()
    near_out[...] = near[...]
    m2l_gather(window, lists[...], gathered)
    fetch.wait()
    result = jnp.dot(held[...], gathered[...], preferred_element_type=f32)
    alive = alive_lanes(live[0], lists.shape[1], result.shape)
    out[...] = jnp.where(alive, result, f32(0.0))


def m2l(live, window, lists, ops, near):
    surface = window.shape[0]
    wide = lists.shape[1] * Q
    vmem = pl.BlockSpec(memory_space=pltpu.VMEM)
    return pl.pallas_call(
        m2l_kernel,
        out_shape=(
            jax.ShapeDtypeStruct((surface, wide), f32),
            jax.ShapeDtypeStruct(near.shape, f32),
        ),
        in_specs=[pl.BlockSpec(memory_space=pltpu.SMEM)] + [vmem] * 2
        + [pl.BlockSpec(memory_space=pl.ANY), vmem],
        out_specs=(vmem, vmem),
        scratch_shapes=[
            pltpu.VMEM((surface * lists.shape[0], wide), bf16),
            pltpu.VMEM(ops.shape, bf16),
            pltpu.SemaphoreType.DMA,
        ],
    )(live, window, lists, ops, near)


def per_device(
    child_dens, users, local_dens, live, m2l_ops, m2l_lists, leaf_pos, leaf_charge, leaf_nbrs
):
    window, near_pot = fused(
        live, child_dens, users, local_dens, leaf_pos, leaf_charge, leaf_nbrs
    )
    return m2l(live, window, m2l_lists, m2l_ops, near_pot)


def solution(mesh):
    placed = (
        P(None, ("gx", "gy")),
        P(("gx", "gy")),
        P(None, ("gx", "gy")),
        P(("gx", "gy")),
        P(),
        P(None, ("gx", "gy")),
        P(None, ("gx", "gy")),
        P(None, ("gx", "gy")),
        P(("gx", "gy"), None),
    )
    return jax.shard_map(
        per_device,
        mesh=mesh,
        in_specs=placed,
        out_specs=(P(None, ("gx", "gy")), P(None, ("gx", "gy"))),
        check_vma=False,
    )
```

profile of v0, /device:TPU:0, one launch (start us, length us, event | category | flops | bytes accessed | tf_op | source)
XLA Modules:
  0.0 25.0 jit_solution(9993489379261610633)
XLA Ops:
  1.3 19.5 %shard_map.104 = (bf16[296,576]{1,0:T(8,128)(2,1)}, f32[4,4096]{1,0:T(4,128)}) custom-call(s32[1]{0:T(128)S(6)} %copy.11.live, bf16[296,256]{1,0:T(8,128)(2,1)} %child.1, s32[1,64]{1,0:T(1,128)} %bitcast.3, bf16[296,512]{1,0:T(8,128)(2,1)} %local.1, f32[3,4096]{1,0:T(4,128)} %pos.1, f32[4,4096]{1,0:T(4,128)} %charge.1, s32[27,128]{1,0:T(8,128)} %bitcast.2), custom_call_target="tpu_custom_call" | custom-call | tf_op jit(solution)/shard_map/pallas_call | solution.py:356
  20.8 4.2 %shard_map.105 = (f32[296,512]{1,0:T(8,128)}, f32[4,4096]{1,0:T(4,128)}) custom-call(s32[1]{0:T(128)S(6)} %copy.11.live, bf16[296,576]{1,0:T(8,128)(2,1)} %get-tuple-element.4.window, s32[8,128]{1,0:T(8,128)} %lists.1, bf16[296,2368]{1,0:T(8,128)(2,1)} %ops.1, f32[4,4096]{1,0:T(4,128)} %get-tuple-element.5.near), custom_call_target="tpu_custom_call" | custom-call | tf_op jit(solution)/shard_map/pallas_call | solution.py:405
where the time goes:
time: 25.2 us; the launch traced here: 25 us
  Pallas kernels  23.7 us (94%)
  between operations  1.29 us (5%)
    pallas_call x1, Pallas kernels, fused(): pl.pallas_call(functools.partial(fused_kernel, nx, ny), out_shape=(jax.Sh...  19.5 us
    pallas_call x1, Pallas kernels, m2l(): pl.pallas_call(m2l_kernel, out_shape=(jax.ShapeDtypeStruct((surface, wide...  4.17 us

commit v1 on v0

--- a/solution.py
+++ b/solution.py
@@ -187,6 +187,19 @@
 def fused_kernel(
     nx,
     ny,
+    live_in,
+    child_in,
+    users_in,
+    local_in,
+    pos_in,
+    charge_in,
+    nbrs_in,
+    lists_in,
+    ops_in,
+    window,
+    out,
+    lists,
+    ops,
     live,
     child,
     users,
@@ -194,12 +207,11 @@
     pos,
     charge,
     nbrs,
-    window,
-    out,
     send1,
     recv1,
     send2,
     recv2,
+    recv3,
     spread,
     first,
     last,
@@ -214,21 +226,43 @@
     sources,
     targets,
     counts,
+    load_sem,
     send_sem,
     recv_sem,
 ):
     mx, my = lax.axis_index("gx"), lax.axis_index("gy")
     total = nx * ny
     me = mx * ny + my
-    after, before = lax.rem(me + 1, total), lax.rem(me + total - 1, total)
-    after = (after // ny, lax.rem(after, ny))
-    before = (before // ny, lax.rem(before, ny))
+    has_low = me > 0
+    has_high = me < total - 1
+
+    def place(rank):
+        return rank // ny, lax.rem(rank, ny)
+
+    after = place(lax.rem(me + 1, total))
+    before = place(lax.rem(me + total - 1, total))
     along_y = [(mx, lax.rem(my + d, ny)) for d in range(1, ny)]
     along_x = [(lax.rem(mx + d, nx), my) for d in range(1, nx)]
 
     barrier = pltpu.get_barrier_semaphore()
-    for device in along_y + along_x + [after, before]:
+
+    def greet(device):
         pl.semaphore_signal(barrier, inc=1, device_id=device, device_id_type=MESH)
+
+    for device in along_x + along_y:
+        greet(device)
+    pl.when(has_low)(lambda: greet(before))
+    pl.when(has_high)(lambda: greet(after))
+
+    def load(k, src, dst):
+        copy = pltpu.make_async_copy(src, dst, load_sem.at[k])
+        copy.start()
+        return copy
+
+    load_child = [load(0, child_in, child), load(1, users_in, users)]
+    load_leaf = [load(2, pos_in, pos), load(3, charge_in, charge), load(4, nbrs_in, nbrs)]
+    load_local = [load(5, local_in, local), load(6, live_in, live)]
+    load_ops = [load(7, lists_in, lists), load(8, ops_in, ops)]
 
     surface, wide = local.shape
     slots = wide // Q
@@ -237,15 +271,42 @@
     count = pos.shape[1]
     own = SH_DEV * Q
     message = nx * own
+    for copy in load_child:
+        copy.wait()
     partial_sums(child, users, send1, nx, ny)
-    alive = alive_lanes(live[0], slots, (surface, wide))
-    owned = jnp.where(alive, local[...].astype(f32), f32(0.0)).astype(bf16)
-    last[...] = owned[:, wide - rim :]
-    pl.semaphore_wait(barrier, len(along_y) + len(along_x) + 2)
+    for copy in load_leaf:
+        copy.wait()
+    coords[...] = jnp.zeros_like(coords)
+    coords[0:3, halo : halo + count] = pos[...]
+    charges[:, halo : halo + count] = charge[...]
+    mine = coords[:, halo : halo + count]
+    sources[halo : halo + count, :] = source_rows(mine).T
+    targets[...] = target_rows(mine)
+    near_counts(nbrs[...], counts)
+    for copy in load_local:
+        copy.wait()
+    last[...] = local[:, wide - rim :]
+    first[...] = local[:, 0:rim]
+
+    groups = counts.shape[0]
+    skip = halo // (GROUP * NPT)
+    pairs = (groups - 2 * skip) // 2
+
+    def step(p, carry):
+        for g in range(2):
+            near_group(skip + 2 * p + g, sources, targets, charges, counts, out)
+        return carry
+
+    early = jnp.where(me == 0, 3, jnp.where(me == 1, 2, jnp.where(me < ny, 1, 0)))
+    early = jnp.minimum(early, pairs)
+    half = jnp.minimum(early + (pairs + 1) // 2, pairs)
+    lax.fori_loop(0, early, step, 0)
+    neighbours = jnp.where(has_low, 1, 0) + jnp.where(has_high, 1, 0)
+    pl.semaphore_wait(barrier, len(along_y) + len(along_x) + neighbours)
 
     at = [0]
 
-    def remote(src, dst, device):
+    def remote(src, dst, device, sends=None, takes=None):
         k = at[0]
         at[0] += 1
         copy = pltpu.make_async_remote_copy(
@@ -256,8 +317,16 @@
             device_id=device,
             device_id_type=MESH,
         )
-        copy.start()
-        return copy
+        if sends is None:
+            copy.start()
+            return copy.wait
+        pl.when(sends)(copy.start)
+
+        def wait():
+            pl.when(sends)(copy.wait_send)
+            pl.when(takes)(copy.wait_recv)
+
+        return wait
 
     step1 = []
     for d in range(1, ny):
@@ -266,83 +335,89 @@
             remote(send1.at[pl.ds(start, message), :], recv1.at[d - 1], along_y[d - 1])
         )
     leaf = [
-        remote(pos.at[:, count - halo : count], pos_low, after),
-        remote(charge.at[:, count - halo : count], charge_low, after),
-        remote(pos.at[:, 0:halo], pos_high, before),
-        remote(charge.at[:, 0:halo], charge_high, before),
+        remote(pos.at[:, count - halo : count], pos_low, after, has_high, has_low),
+        remote(charge.at[:, count - halo : count], charge_low, after, has_high, has_low),
+        remote(pos.at[:, 0:halo], pos_high, before, has_low, has_high),
+        remote(charge.at[:, 0:halo], charge_high, before, has_low, has_high),
     ]
-    rims = [remote(last, low, after)]
-
-    coords[...] = jnp.zeros_like(coords)
-    coords[0:3, halo : halo + count] = pos[...]
-    charges[:, halo : halo + count] = charge[...]
-    mine = coords[:, halo : halo + count]
-    sources[halo : halo + count, :] = source_rows(mine).T
-    targets[...] = target_rows(mine)
-    near_counts(nbrs[...], counts)
-    groups = counts.shape[0]
-    skip = halo // (GROUP * NPT)
-
-    def step(g, carry):
-        near_group(g, sources, targets, charges, counts, out)
-        return carry
-
-    third = (groups - 2 * skip) // 3
-    lax.fori_loop(skip, skip + third, step, 0, unroll=4)
-
-    for copy in step1:
-        copy.wait()
+    rims = [
+        remote(last, low, after, has_high, has_low),
+        remote(first, high, before, has_low, has_high),
+    ]
+
+    lax.fori_loop(early, half, step, 0)
+
+    for wait in step1:
+        wait()
     value = send1[pl.ds(pl.multiple_of(my * message, message), message), :]
     for d in range(ny - 1):
         value = value + recv1[d]
     for k in range(nx):
         send2[k] = value[k * own : (k + 1) * own]
     step2 = []
-    for d in range(1, nx):
-        step2.append(remote(send2.at[lax.rem(mx + d, nx)], recv2.at[d - 1], along_x[d - 1]))
-
-    lax.fori_loop(skip + third, skip + 2 * third, step, 0, unroll=4)
-
-    for copy in step2:
+    for d in range(nx):
+        row = lax.rem(mx + d, nx)
+        rank = row * ny + my
+        left = place(lax.rem(rank + total - 1, total))
+        step2.append(remote(send2.at[row], recv3.at[d], left, rank > 0, has_high))
+        if d > 0:
+            step2.append(remote(send2.at[row], recv2.at[d - 1], along_x[d - 1]))
+
+    lax.fori_loop(half, pairs, step, 0)
+
+    alive = alive_lanes(live[...], slots, (surface, wide))
+    owned = jnp.where(alive, local[...].astype(f32), f32(0.0))
+    lanes = spread.shape[0]
+    window[:, rim + lanes : rim + wide] = owned[:, lanes:].astype(bf16)
+
+    for wait in leaf:
+        wait()
+    for pos_ref, charge_ref, start, there in (
+        (pos_low, charge_low, 0, has_low),
+        (pos_high, charge_high, halo + count, has_high),
+    ):
+        span = slice(start, start + halo)
+        coords[0:3, span] = jnp.where(there, pos_ref[...], f32(0.0))
+        charges[:, span] = jnp.where(there, charge_ref[...], f32(0.0))
+        sources[span, :] = source_rows(coords[:, span]).T
+
+    def edge(p, carry):
+        for g in range(2):
+            at_low = 2 * p + g
+            g = jnp.where(at_low < skip, at_low, groups - 2 * skip + at_low)
+            near_group(g, sources, targets, charges, counts, out)
+        return carry
+
+    lax.fori_loop(0, skip, edge, 0)
+
+    for copy in load_ops:
         copy.wait()
+    for wait in rims:
+        wait()
+    window[:, 0:rim] = jnp.where(has_low, low[...], jnp.zeros_like(low))
+    for wait in step2:
+        wait()
     shared = send2[mx]
     for d in range(nx - 1):
         shared = shared + recv2[d]
     spread[...] = jnp.zeros_like(spread)
     spread[0:own, :] = shared
-    lanes = spread.shape[0]
-    front = local[:, 0:lanes].astype(f32) + spread[...].T
+    front = owned[:, 0:lanes] + spread[...].T
     front = jnp.where(alive[:, 0:lanes], front, f32(0.0)).astype(bf16)
-    first[...] = front[:, 0:rim]
-    rims.append(remote(first, high, before))
     window[:, rim : rim + lanes] = front
-    window[:, rim + lanes : rim + wide] = owned[:, lanes:]
-
-    lax.fori_loop(skip + 2 * third, groups - skip, step, 0, unroll=4)
-
-    for copy in leaf:
-        copy.wait()
-    has_low = me > 0
-    has_high = me < total - 1
-    for pos_ref, charge_ref, start, there in (
-        (pos_low, charge_low, 0, has_low),
-        (pos_high, charge_high, halo + count, has_high),
-    ):
-        span = slice(start, start + halo)
-        coords[0:3, span] = pos_ref[...]
-        charges[:, span] = jnp.where(there, charge_ref[...], f32(0.0))
-        sources[span, :] = source_rows(coords[:, span]).T
-    lax.fori_loop(0, skip, step, 0, unroll=2)
-    lax.fori_loop(groups - skip, groups, step, 0, unroll=2)
-
-    for copy in rims:
-        copy.wait()
-    window[:, 0:rim] = jnp.where(has_low, low[...], jnp.zeros_like(low))
-    window[:, rim + wide :] = jnp.where(has_high, high[...], jnp.zeros_like(high))
-
-
-def fused(live, child, users, local, pos, charge, nbrs):
+    shared = recv3[0]
+    for d in range(1, nx):
+        shared = shared + recv3[d]
+    spread[0:own, :] = shared
+    front = high[...].astype(f32) + spread[...].T[:, 0:rim]
+    window[:, rim + wide :] = jnp.where(has_high, front, f32(0.0)).astype(bf16)
+
+
+def fused(live, child, users, local, pos, charge, nbrs, lists, ops):
     nx, ny = lax.axis_size("gx"), lax.axis_size("gy")
+    users = users.reshape(-1, 64)
+    nbrs = nbrs.T
+    live = live.reshape(1, 1)
     surface, wide = local.shape
     count = pos.shape[1]
     halo = HL * NPT
@@ -351,21 +426,27 @@
     reach = (GROUP + 2 * HL) * NPT
     rim = wide // 16
     own = SH_DEV * Q
-    copies = ny - 1 + nx - 1 + 6
+    copies = ny - 1 + 2 * nx - 1 + 6
     vmem = pl.BlockSpec(memory_space=pltpu.VMEM)
+    inputs = (live, child, users, local, pos, charge, nbrs, lists, ops)
+    inputs = [live] + [pltpu.with_memory_space_constraint(x, pltpu.HBM) for x in inputs[1:]]
     return pl.pallas_call(
         functools.partial(fused_kernel, nx, ny),
         out_shape=(
             jax.ShapeDtypeStruct((surface, wide + 2 * rim), bf16),
             jax.ShapeDtypeStruct(charge.shape, f32),
+            jax.ShapeDtypeStruct(lists.shape, lists.dtype),
+            jax.ShapeDtypeStruct(ops.shape, ops.dtype),
         ),
-        in_specs=[pl.BlockSpec(memory_space=pltpu.SMEM)] + [vmem] * 6,
-        out_specs=(vmem, vmem),
-        scratch_shapes=[
+        in_specs=[pl.BlockSpec(memory_space=pltpu.HBM)] * len(inputs),
+        out_specs=(vmem,) * 4,
+        scratch_shapes=[pltpu.VMEM(x.shape, x.dtype) for x in inputs[:7]]
+        + [
             pltpu.VMEM((ny * nx * own, surface), f32),
             pltpu.VMEM((ny - 1, nx * own, surface), f32),
             pltpu.VMEM((nx, own, surface), f32),
             pltpu.VMEM((nx - 1, own, surface), f32),
+            pltpu.VMEM((nx, own, surface), f32),
             pltpu.VMEM((128, surface), f32),
             pltpu.VMEM((surface, rim), bf16),
             pltpu.VMEM((surface, rim), bf16),
@@ -380,52 +461,63 @@
             pltpu.VMEM((span, 64), bf16),
             pltpu.VMEM((64, count), bf16),
             pltpu.VMEM((groups, GROUP, reach), f32),
+            pltpu.SemaphoreType.DMA((len(inputs),)),
             pltpu.SemaphoreType.DMA((copies,)),
             pltpu.SemaphoreType.DMA((copies,)),
         ],
-        compiler_params=pltpu.CompilerParams(collective_id=0, has_side_effects=True),
-    )(live, child, users.reshape(-1, 64), local, pos, charge, nbrs.T)
-
-
-def m2l_kernel(live, window, lists, ops, near, out, near_out, gathered, held, sem):
-    fetch = pltpu.make_async_copy(ops, held, sem)
-    fetch.start()
-    near_out[...] = near[...]
+        compiler_params=pltpu.CompilerParams(
+            collective_id=0, has_side_effects=True, vmem_limit_bytes=32 * 2**20
+        ),
+    )(*inputs)
+
+
+def m2l_kernel(live, window, lists, ops, near, out, near_out, gathered, result, sem):
+    send = pltpu.make_async_copy(near, near_out, sem.at[0])
+    send.start()
     m2l_gather(window, lists[...], gathered)
-    fetch.wait()
-    result = jnp.dot(held[...], gathered[...], preferred_element_type=f32)
-    alive = alive_lanes(live[0], lists.shape[1], result.shape)
-    out[...] = jnp.where(alive, result, f32(0.0))
+    surface, wide = result.shape
+    alive = alive_lanes(live[...], lists.shape[1], result.shape)
+    copies = [send]
+    for k in range(2):
+        part = slice(k * wide // 2, (k + 1) * wide // 2)
+        value = jnp.dot(ops[...], gathered[:, part], preferred_element_type=f32)
+        result[:, part] = jnp.where(alive[:, part], value, f32(0.0))
+        copy = pltpu.make_async_copy(result.at[:, part], out.at[:, part], sem.at[1 + k])
+        copy.start()
+        copies.append(copy)
+    for copy in copies:
+        copy.wait()
 
 
 def m2l(live, window, lists, ops, near):
     surface = window.shape[0]
     wide = lists.shape[1] * Q
     vmem = pl.BlockSpec(memory_space=pltpu.VMEM)
+    hbm = pl.BlockSpec(memory_space=pltpu.HBM)
     return pl.pallas_call(
         m2l_kernel,
         out_shape=(
             jax.ShapeDtypeStruct((surface, wide), f32),
             jax.ShapeDtypeStruct(near.shape, f32),
         ),
-        in_specs=[pl.BlockSpec(memory_space=pltpu.SMEM)] + [vmem] * 2
-        + [pl.BlockSpec(memory_space=pl.ANY), vmem],
-        out_specs=(vmem, vmem),
+        in_specs=[vmem] * 5,
+        out_specs=(hbm, hbm),
         scratch_shapes=[
             pltpu.VMEM((surface * lists.shape[0], wide), bf16),
-            pltpu.VMEM(ops.shape, bf16),
-            pltpu.SemaphoreType.DMA,
+            pltpu.VMEM((surface, wide), f32),
+            pltpu.SemaphoreType.DMA((3,)),
         ],
-    )(live, window, lists, ops, near)
+        compiler_params=pltpu.CompilerParams(vmem_limit_bytes=24 * 2**20),
+    )(live.reshape(1, 1), window, lists, ops, near)
 
 
 def per_device(
     child_dens, users, local_dens, live, m2l_ops, m2l_lists, leaf_pos, leaf_charge, leaf_nbrs
 ):
-    window, near_pot = fused(
-        live, child_dens, users, local_dens, leaf_pos, leaf_charge, leaf_nbrs
+    window, near_pot, lists, ops = fused(
+        live, child_dens, users, local_dens, leaf_pos, leaf_charge, leaf_nbrs, m2l_lists, m2l_ops
     )
-    return m2l(live, window, m2l_lists, m2l_ops, near_pot)
+    return m2l(live, window, lists, ops, near_pot)
 
 
 def solution(mesh):

time: 25.2 us -> 18.9 us (0.75)
  Pallas kernels: 23.7 us -> 17.5 us
    pallas_call x1, Pallas kernels: 19.5 us -> 14.8 us  [fused(): pl.pallas_call(functools.partial(fused_kernel, nx, ny), out_shape=(jax.Sh...]
    pallas_call x1, Pallas kernels: 4.17 us -> 2.67 us  [m2l(): pl.pallas_call(m2l_kernel, out_shape=(jax.ShapeDtypeStruct((surface, wide...]
where the time goes in v1:
time: 18.9 us; the launch traced here: 18.8 us
  Pallas kernels  17.5 us (93%)
  between operations  1.29 us (7%)
    pallas_call x1, Pallas kernels, fused(): pl.pallas_call(functools.partial(fused_kernel, nx, ny), out_shape=(jax.Sh...  14.8 us
    pallas_call x1, Pallas kernels, m2l(): pl.pallas_call(m2l_kernel, out_shape=(jax.ShapeDtypeStruct((surface, wide...  2.67 us

profile of v1, /device:TPU:0, one launch (start us, length us, event | category | flops | bytes accessed | tf_op | source)
XLA Modules:
  0.0 18.8 jit_solution(755307447901159293)
XLA Ops:
  1.3 14.8 %shard_map.104 = (bf16[296,576]{1,0:T(8,128)(2,1)S(1)}, f32[4,4096]{1,0:T(4,128)S(1)}, s32[8,128]{1,0:T(8,128)S(1)}, bf16[296,2368]{1,0:T(8,128)(2,1)S(1)}) custom-call(s32[1,1]{1,0:T(1,128)} %bitcast.3.live_in, bf16[296,256]{1,0:T(8,128)(2,1)} %child_in.1, s32[1,64]{1,0:T(1,128)} %bitcast.6, bf16[296,512]{1,0:T(8,128)(2,1)} %local_in.1, f32[3,4096]{1,0:T(4,128)} %pos_in.1, ...), custom_call_target="tpu_custom_call" | custom-call | tf_op jit(solution)/shard_map/pallas_call | solution.py:433
  16.1 2.7 %shard_map.105 = (f32[296,512]{1,0:T(8,128)}, f32[4,4096]{1,0:T(4,128)}) custom-call(s32[1,1]{1,0:T(1,128)} %bitcast.4.live, bf16[296,576]{1,0:T(8,128)(2,1)S(1)} %get-tuple-element.6.window, s32[8,128]{1,0:T(8,128)S(1)} %get-tuple-element.7.lists, bf16[296,2368]{1,0:T(8,128)(2,1)S(1)} %get-tuple-element.8.ops, f32[4,4096]{1,0:T(4,128)S(1)} %get-tuple-element.9.near), custom_call_target="tpu_custom_call" | custom-call | tf_op jit(solution)/shard_map/pallas_call | solution.py:497

commit v2 on v1

--- a/solution.py
+++ b/solution.py
@@ -14,6 +14,7 @@
 HL = 16
 GROUP = 8
 BLOCK = 32
+LANES = 128
 
 soften = 0.01
 f32 = jnp.float32
@@ -102,6 +103,7 @@
     wl = (w - wh.astype(f32)).astype(bf16)
     w = jnp.concatenate([wh, wl], axis=0)
     total = jnp.zeros((2 * rows, size), f32)
+    rest = jnp.zeros((rows, size), f32)
     for at in range(0, reach, 256):
         width = min(256, reach - at)
         left = sources[pl.ds(pl.multiple_of(start + at, size), width), :]
@@ -110,8 +112,8 @@
         low = (kernel - high.astype(f32)).astype(bf16)
         span = slice(at, at + width)
         total = total + jnp.dot(w[:, span], high, preferred_element_type=f32)
-        total = total + jnp.dot(w[:, span], low, preferred_element_type=f32)
-    flat = total[:rows] + total[rows:]
+        rest = rest + jnp.dot(wh[:, span], low, preferred_element_type=f32)
+    flat = total[:rows] + total[rows:] + rest
     mine = row_ids(flat.shape) % GROUP == lane_ids(flat.shape) // NPT
     flat = jnp.where(mine, flat, f32(0.0))
     out[:, pl.ds(start, size)] = jnp.sum(flat.reshape(Q, GROUP, size), axis=1)
@@ -123,7 +125,7 @@
     return (slot < lower) | (slot >= slots - (live - lower))
 
 
-def m2l_gather(window, lists, gathered):
+def m2l_gather(window, lists, gathered, blocks):
     offsets, slots = lists.shape
     surface = window.shape[0]
     wide = slots * Q
@@ -136,7 +138,7 @@
     place = (place - 1) * Q + lane_ids(place.shape) % Q
     size = BLOCK * Q
     depth = (BLOCK + slots // 8) * Q
-    for b in range(slots // BLOCK):
+    for i, b in enumerate(blocks):
         block = window[:, b * size : b * size + depth]
         ids = row_ids((depth, size)) + b * size
         for o in range(0, offsets, 2):
@@ -146,12 +148,30 @@
             hot = jnp.concatenate([jnp.where(hit, f32(1.0), f32(0.0)) for hit in hits], axis=1)
             pair = jnp.dot(block, hot.astype(bf16), preferred_element_type=f32)
             both = jnp.concatenate([pair[:, :size], pair[:, size:]], axis=0).astype(bf16)
-            gathered[o * surface : (o + 2) * surface, b * size : (b + 1) * size] = both
-
-
-def partial_sums(child, users, send, nx, ny):
+            gathered[o * surface : (o + 2) * surface, i * size : (i + 1) * size] = both
+
+
+def packed_rows(message, surface):
+    whole = surface // LANES
+    tail = surface - whole * LANES
+    assert tail <= LANES // 2
+    return whole * message + (message // 2 if tail else 0)
+
+
+def unpack(value, message, surface):
+    whole = surface // LANES
+    tail = surface - whole * LANES
+    parts = [value[c * message : (c + 1) * message] for c in range(whole)]
+    if tail:
+        end = value[whole * message :]
+        middle = LANES // 2
+        parts.append(jnp.concatenate([end[:, :tail], end[:, middle : middle + tail]], axis=0))
+    return jnp.concatenate(parts, axis=1)
+
+
+def partial_sums(child, users, total, send, nx, ny):
     own = SH_DEV * Q
-    rows = send.shape[0]
+    rows, surface = total.shape
     chunks, count = users.shape
     wide = count * Q
     row = row_ids((rows, wide))
@@ -174,14 +194,28 @@
             hot, block, (((1,), (1,)), ((), ())), preferred_element_type=f32
         )
 
-    send[...] = chunk_sum(0)
+    total[...] = chunk_sum(0)
     if chunks > 1:
 
         def step(i, carry):
-            send[...] += chunk_sum(i)
+            total[...] += chunk_sum(i)
             return carry
 
         lax.fori_loop(1, chunks, step, 0)
+    message = nx * own
+    half = message // 2
+    whole = surface // LANES
+    tail = surface - whole * LANES
+    for k in range(ny):
+        block = total[k * message : (k + 1) * message, :]
+        for c in range(whole):
+            send[k, c * message : (c + 1) * message, :] = block[:, c * LANES : (c + 1) * LANES]
+        if tail:
+            gap = jnp.zeros((half, LANES // 2 - tail), f32)
+            end = block[:, whole * LANES :]
+            send[k, whole * message :, :] = jnp.concatenate(
+                [end[:half], gap, end[half:], gap], axis=1
+            )
 
 
 def fused_kernel(
@@ -198,6 +232,7 @@
     ops_in,
     window,
     out,
+    inner,
     lists,
     ops,
     live,
@@ -207,6 +242,7 @@
     pos,
     charge,
     nbrs,
+    sums,
     send1,
     recv1,
     send2,
@@ -226,6 +262,7 @@
     sources,
     targets,
     counts,
+    gathered,
     load_sem,
     send_sem,
     recv_sem,
@@ -261,8 +298,6 @@
 
     load_child = [load(0, child_in, child), load(1, users_in, users)]
     load_leaf = [load(2, pos_in, pos), load(3, charge_in, charge), load(4, nbrs_in, nbrs)]
-    load_local = [load(5, local_in, local), load(6, live_in, live)]
-    load_ops = [load(7, lists_in, lists), load(8, ops_in, ops)]
 
     surface, wide = local.shape
     slots = wide // Q
@@ -273,34 +308,54 @@
     message = nx * own
     for copy in load_child:
         copy.wait()
-    partial_sums(child, users, send1, nx, ny)
+    partial_sums(child, users, sums, send1, nx, ny)
+    load_local = [load(5, local_in, local), load(6, live_in, live)]
+    load_ops = [load(7, lists_in, lists), load(8, ops_in, ops)]
+
+    def prepare():
+        coords[...] = jnp.zeros_like(coords)
+        coords[0:3, halo : halo + count] = pos[...]
+        charges[:, halo : halo + count] = charge[...]
+        mine = coords[:, halo : halo + count]
+        sources[halo : halo + count, :] = source_rows(mine).T
+        targets[...] = target_rows(mine)
+        near_counts(nbrs[...], counts)
+
     for copy in load_leaf:
         copy.wait()
-    coords[...] = jnp.zeros_like(coords)
-    coords[0:3, halo : halo + count] = pos[...]
-    charges[:, halo : halo + count] = charge[...]
-    mine = coords[:, halo : halo + count]
-    sources[halo : halo + count, :] = source_rows(mine).T
-    targets[...] = target_rows(mine)
-    near_counts(nbrs[...], counts)
-    for copy in load_local:
-        copy.wait()
-    last[...] = local[:, wide - rim :]
-    first[...] = local[:, 0:rim]
-
     groups = counts.shape[0]
     skip = halo // (GROUP * NPT)
-    pairs = (groups - 2 * skip) // 2
+    quads = (groups - 2 * skip) // 4
 
     def step(p, carry):
-        for g in range(2):
-            near_group(skip + 2 * p + g, sources, targets, charges, counts, out)
+        for g in range(4):
+            near_group(skip + 4 * p + g, sources, targets, charges, counts, out)
         return carry
 
-    early = jnp.where(me == 0, 3, jnp.where(me == 1, 2, jnp.where(me < ny, 1, 0)))
-    early = jnp.minimum(early, pairs)
-    half = jnp.minimum(early + (pairs + 1) // 2, pairs)
-    lax.fori_loop(0, early, step, 0)
+    early = me < ny + 1
+
+    def ahead():
+        prepare()
+        step(0, 0)
+
+    def middle():
+        for copy in load_local:
+            copy.wait()
+        last[...] = local[:, wide - rim :]
+        first[...] = local[:, 0:rim]
+        alive = alive_lanes(live[...], slots, (surface, wide))
+        owned = jnp.where(alive, local[...].astype(f32), f32(0.0))
+        window[:, rim : rim + wide] = owned.astype(bf16)
+        for copy in load_ops:
+            copy.wait()
+        blocks = slots // BLOCK
+        size = BLOCK * Q
+        m2l_gather(window, lists[...], gathered, range(1, blocks - 1))
+        value = jnp.dot(ops[...], gathered[...], preferred_element_type=f32)
+        inner[...] = jnp.where(alive[:, size : wide - size], value, f32(0.0))
+
+    pl.when(early)(ahead)
+    pl.when(me == 0)(middle)
     neighbours = jnp.where(has_low, 1, 0) + jnp.where(has_high, 1, 0)
     pl.semaphore_wait(barrier, len(along_y) + len(along_x) + neighbours)
 
@@ -330,28 +385,24 @@
 
     step1 = []
     for d in range(1, ny):
-        start = pl.multiple_of(lax.rem(my + d, ny) * message, message)
-        step1.append(
-            remote(send1.at[pl.ds(start, message), :], recv1.at[d - 1], along_y[d - 1])
-        )
+        step1.append(remote(send1.at[lax.rem(my + d, ny)], recv1.at[d - 1], along_y[d - 1]))
     leaf = [
         remote(pos.at[:, count - halo : count], pos_low, after, has_high, has_low),
         remote(charge.at[:, count - halo : count], charge_low, after, has_high, has_low),
         remote(pos.at[:, 0:halo], pos_high, before, has_low, has_high),
         remote(charge.at[:, 0:halo], charge_high, before, has_low, has_high),
     ]
-    rims = [
-        remote(last, low, after, has_high, has_low),
-        remote(first, high, before, has_low, has_high),
-    ]
-
-    lax.fori_loop(early, half, step, 0)
+    pl.when(jnp.logical_not(early))(ahead)
+    pl.when(me > 0)(middle)
+    half = jnp.where(me < 2, quads, jnp.where(early, jnp.minimum(2, quads), 1))
+    lax.fori_loop(1, half, step, 0)
 
     for wait in step1:
         wait()
-    value = send1[pl.ds(pl.multiple_of(my * message, message), message), :]
+    value = send1[my]
     for d in range(ny - 1):
         value = value + recv1[d]
+    value = unpack(value, message, surface)
     for k in range(nx):
         send2[k] = value[k * own : (k + 1) * own]
     step2 = []
@@ -363,12 +414,15 @@
         if d > 0:
             step2.append(remote(send2.at[row], recv2.at[d - 1], along_x[d - 1]))
 
-    lax.fori_loop(half, pairs, step, 0)
-
-    alive = alive_lanes(live[...], slots, (surface, wide))
-    owned = jnp.where(alive, local[...].astype(f32), f32(0.0))
+    rims = [
+        remote(last, low, after, has_high, has_low),
+        remote(first, high, before, has_low, has_high),
+    ]
+
+    lax.fori_loop(half, quads, step, 0)
+
     lanes = spread.shape[0]
-    window[:, rim + lanes : rim + wide] = owned[:, lanes:].astype(bf16)
+    alive = alive_lanes(live[...], slots, (surface, lanes))
 
     for wait in leaf:
         wait()
@@ -381,17 +435,9 @@
         charges[:, span] = jnp.where(there, charge_ref[...], f32(0.0))
         sources[span, :] = source_rows(coords[:, span]).T
 
-    def edge(p, carry):
-        for g in range(2):
-            at_low = 2 * p + g
-            g = jnp.where(at_low < skip, at_low, groups - 2 * skip + at_low)
-            near_group(g, sources, targets, charges, counts, out)
-        return carry
-
-    lax.fori_loop(0, skip, edge, 0)
-
-    for copy in load_ops:
-        copy.wait()
+    for g in list(range(skip)) + list(range(groups - skip, groups)):
+        near_group(g, sources, targets, charges, counts, out)
+
     for wait in rims:
         wait()
     window[:, 0:rim] = jnp.where(has_low, low[...], jnp.zeros_like(low))
@@ -402,8 +448,8 @@
         shared = shared + recv2[d]
     spread[...] = jnp.zeros_like(spread)
     spread[0:own, :] = shared
-    front = owned[:, 0:lanes] + spread[...].T
-    front = jnp.where(alive[:, 0:lanes], front, f32(0.0)).astype(bf16)
+    front = local[:, 0:lanes].astype(f32) + spread[...].T
+    front = jnp.where(alive, front, f32(0.0)).astype(bf16)
     window[:, rim : rim + lanes] = front
     shared = recv3[0]
     for d in range(1, nx):
@@ -426,6 +472,7 @@
     reach = (GROUP + 2 * HL) * NPT
     rim = wide // 16
     own = SH_DEV * Q
+    packed = packed_rows(nx * own, surface)
     copies = ny - 1 + 2 * nx - 1 + 6
     vmem = pl.BlockSpec(memory_space=pltpu.VMEM)
     inputs = (live, child, users, local, pos, charge, nbrs, lists, ops)
@@ -435,15 +482,17 @@
         out_shape=(
             jax.ShapeDtypeStruct((surface, wide + 2 * rim), bf16),
             jax.ShapeDtypeStruct(charge.shape, f32),
+            jax.ShapeDtypeStruct((surface, wide - 2 * BLOCK * Q), f32),
             jax.ShapeDtypeStruct(lists.shape, lists.dtype),
             jax.ShapeDtypeStruct(ops.shape, ops.dtype),
         ),
         in_specs=[pl.BlockSpec(memory_space=pltpu.HBM)] * len(inputs),
-        out_specs=(vmem,) * 4,
+        out_specs=(vmem,) * 5,
         scratch_shapes=[pltpu.VMEM(x.shape, x.dtype) for x in inputs[:7]]
         + [
             pltpu.VMEM((ny * nx * own, surface), f32),
-            pltpu.VMEM((ny - 1, nx * own, surface), f32),
+            pltpu.VMEM((ny, packed, LANES), f32),
+            pltpu.VMEM((ny - 1, packed, LANES), f32),
             pltpu.VMEM((nx, own, surface), f32),
             pltpu.VMEM((nx - 1, own, surface), f32),
             pltpu.VMEM((nx, own, surface), f32),
@@ -461,6 +510,7 @@
             pltpu.VMEM((span, 64), bf16),
             pltpu.VMEM((64, count), bf16),
             pltpu.VMEM((groups, GROUP, reach), f32),
+            pltpu.VMEM((surface * lists.shape[0], wide - 2 * BLOCK * Q), bf16),
             pltpu.SemaphoreType.DMA((len(inputs),)),
             pltpu.SemaphoreType.DMA((copies,)),
             pltpu.SemaphoreType.DMA((copies,)),
@@ -471,27 +521,33 @@
     )(*inputs)
 
 
-def m2l_kernel(live, window, lists, ops, near, out, near_out, gathered, result, sem):
-    send = pltpu.make_async_copy(near, near_out, sem.at[0])
-    send.start()
-    m2l_gather(window, lists[...], gathered)
-    surface, wide = result.shape
-    alive = alive_lanes(live[...], lists.shape[1], result.shape)
-    copies = [send]
-    for k in range(2):
-        part = slice(k * wide // 2, (k + 1) * wide // 2)
-        value = jnp.dot(ops[...], gathered[:, part], preferred_element_type=f32)
-        result[:, part] = jnp.where(alive[:, part], value, f32(0.0))
-        copy = pltpu.make_async_copy(result.at[:, part], out.at[:, part], sem.at[1 + k])
+def m2l_kernel(live, window, lists, ops, near, inner, out, near_out, gathered, result, sem):
+    surface, wide = out.shape
+    size = BLOCK * Q
+    copies = []
+
+    def write(src, dst):
+        copy = pltpu.make_async_copy(src, dst, sem.at[len(copies)])
         copy.start()
         copies.append(copy)
+
+    write(inner, out.at[:, size : wide - size])
+    write(near, near_out)
+    m2l_gather(window, lists[...], gathered, (0, lists.shape[1] // BLOCK - 1))
+    alive = alive_lanes(live[...], lists.shape[1], (surface, wide))
+    value = jnp.dot(ops[...], gathered[...], preferred_element_type=f32)
+    for part, start in ((slice(0, size), 0), (slice(size, 2 * size), wide - size)):
+        span = slice(start, start + size)
+        result[:, part] = jnp.where(alive[:, span], value[:, part], f32(0.0))
+        write(result.at[:, part], out.at[:, span])
     for copy in copies:
         copy.wait()
 
 
-def m2l(live, window, lists, ops, near):
+def m2l(live, window, lists, ops, near, inner):
     surface = window.shape[0]
     wide = lists.shape[1] * Q
+    size = BLOCK * Q
     vmem = pl.BlockSpec(memory_space=pltpu.VMEM)
     hbm = pl.BlockSpec(memory_space=pltpu.HBM)
     return pl.pallas_call(
@@ -500,24 +556,24 @@
             jax.ShapeDtypeStruct((surface, wide), f32),
             jax.ShapeDtypeStruct(near.shape, f32),
         ),
-        in_specs=[vmem] * 5,
+        in_specs=[vmem] * 6,
         out_specs=(hbm, hbm),
         scratch_shapes=[
-            pltpu.VMEM((surface * lists.shape[0], wide), bf16),
-            pltpu.VMEM((surface, wide), f32),
-            pltpu.SemaphoreType.DMA((3,)),
+            pltpu.VMEM((surface * lists.shape[0], 2 * size), bf16),
+            pltpu.VMEM((surface, 2 * size), f32),
+            pltpu.SemaphoreType.DMA((4,)),
         ],
         compiler_params=pltpu.CompilerParams(vmem_limit_bytes=24 * 2**20),
-    )(live.reshape(1, 1), window, lists, ops, near)
+    )(live.reshape(1, 1), window, lists, ops, near, inner)
 
 
 def per_device(
     child_dens, users, local_dens, live, m2l_ops, m2l_lists, leaf_pos, leaf_charge, leaf_nbrs
 ):
-    window, near_pot, lists, ops = fused(
+    window, near_pot, inner, lists, ops = fused(
         live, child_dens, users, local_dens, leaf_pos, leaf_charge, leaf_nbrs, m2l_lists, m2l_ops
     )
-    return m2l(live, window, lists, ops, near_pot)
+    return m2l(live, window, lists, ops, near_pot, inner)
 
 
 def solution(mesh):

time: 18.9 us -> 17.9 us (0.947)
  Pallas kernels: 17.5 us -> 16.3 us
    pallas_call x1, Pallas kernels: 14.8 us -> 14 us  [fused(): pl.pallas_call(functools.partial(fused_kernel, nx, ny), out_shape=(jax.Sh...]
    pallas_call x1, Pallas kernels: 2.67 us -> 2.29 us  [m2l(): pl.pallas_call(m2l_kernel, out_shape=(jax.ShapeDtypeStruct((surface, wide...]
where the time goes in v2:
time: 17.9 us; the launch traced here: 17.8 us
  Pallas kernels  16.3 us (91%)
  between operations  1.45 us (8%)
    pallas_call x1, Pallas kernels, fused(): pl.pallas_call(functools.partial(fused_kernel, nx, ny), out_shape=(jax.Sh...  14 us
    pallas_call x1, Pallas kernels, m2l(): pl.pallas_call(m2l_kernel, out_shape=(jax.ShapeDtypeStruct((surface, wide...  2.29 us

profile of v2, /device:TPU:0, one launch (start us, length us, event | category | flops | bytes accessed | tf_op | source)
XLA Modules:
  0.0 17.8 jit_solution(2096532851553621897)
XLA Ops:
  1.3 14.0 %shard_map.104 = (bf16[296,576]{1,0:T(8,128)(2,1)S(1)}, f32[4,4096]{1,0:T(4,128)S(1)}, f32[296,256]{1,0:T(8,128)S(1)}, s32[8,128]{1,0:T(8,128)S(1)}, bf16[296,2368]{1,0:T(8,128)(2,1)S(1)}) custom-call(s32[1,1]{1,0:T(1,128)} %bitcast.3.live_in, bf16[296,256]{1,0:T(8,128)(2,1)} %child_in.1, s32[1,64]{1,0:T(1,128)} %bitcast.6, bf16[296,512]{1,0:T(8,128)(2,1)} %local_in.1, ...), custom_call_target="tpu_custom_call" | custom-call | tf_op jit(solution)/shard_map/pallas_call | solution.py:480
  15.3 2.3 %shard_map.105 = (f32[296,512]{1,0:T(8,128)}, f32[4,4096]{1,0:T(4,128)}) custom-call(s32[1,1]{1,0:T(1,128)} %bitcast.4.live, bf16[296,576]{1,0:T(8,128)(2,1)S(1)} %get-tuple-element.7.window, s32[8,128]{1,0:T(8,128)S(1)} %get-tuple-element.8.lists, bf16[296,2368]{1,0:T(8,128)(2,1)S(1)} %get-tuple-element.9.ops, f32[4,4096]{1,0:T(4,128)S(1)} %get-tuple-element.10.near, ...), custom_call_target="tpu_custom_call" | custom-call | tf_op jit(solution)/shard_map/pallas_call | solution.py:553

commit v3 on v2

--- a/solution.py
+++ b/solution.py
@@ -138,10 +138,10 @@
     place = (place - 1) * Q + lane_ids(place.shape) % Q
     size = BLOCK * Q
     depth = (BLOCK + slots // 8) * Q
-    for i, b in enumerate(blocks):
-        block = window[:, b * size : b * size + depth]
-        ids = row_ids((depth, size)) + b * size
-        for o in range(0, offsets, 2):
+    for o in range(0, offsets, 2):
+        for i, b in enumerate(blocks):
+            block = window[:, b * size : b * size + depth]
+            ids = row_ids((depth, size)) + b * size
             hits = [
                 ids == place[k : k + 1, b * size : (b + 1) * size] for k in (o, o + 1)
             ]
@@ -301,7 +301,8 @@
 
     surface, wide = local.shape
     slots = wide // Q
-    rim = low.shape[1]
+    rim = low.shape[0]
+    lanes = spread.shape[0]
     halo = pos_low.shape[1]
     count = pos.shape[1]
     own = SH_DEV * Q
@@ -332,7 +333,8 @@
             near_group(skip + 4 * p + g, sources, targets, charges, counts, out)
         return carry
 
-    early = me < ny + 1
+    early = me < 2 * ny
+    late = me >= 2 * ny
 
     def ahead():
         prepare()
@@ -341,27 +343,34 @@
     def middle():
         for copy in load_local:
             copy.wait()
-        last[...] = local[:, wide - rim :]
-        first[...] = local[:, 0:rim]
+        side = local[:, 0:lanes].astype(f32).T
+        first[...] = side[0:rim].astype(bf16)
+        side = local[:, wide - lanes :].astype(f32).T
+        last[...] = side[lanes - rim :].astype(bf16)
         alive = alive_lanes(live[...], slots, (surface, wide))
         owned = jnp.where(alive, local[...].astype(f32), f32(0.0))
+        window[:, 0:rim] = jnp.zeros((surface, rim), bf16)
         window[:, rim : rim + wide] = owned.astype(bf16)
         for copy in load_ops:
             copy.wait()
         blocks = slots // BLOCK
+        m2l_gather(window, lists[...], gathered, range(1, blocks - 1))
+
+    def product():
         size = BLOCK * Q
-        m2l_gather(window, lists[...], gathered, range(1, blocks - 1))
+        alive = alive_lanes(live[...], slots, (surface, wide))
         value = jnp.dot(ops[...], gathered[...], preferred_element_type=f32)
         inner[...] = jnp.where(alive[:, size : wide - size], value, f32(0.0))
 
     pl.when(early)(ahead)
     pl.when(me == 0)(middle)
+    pl.when(me == 0)(product)
     neighbours = jnp.where(has_low, 1, 0) + jnp.where(has_high, 1, 0)
     pl.semaphore_wait(barrier, len(along_y) + len(along_x) + neighbours)
 
     at = [0]
 
-    def remote(src, dst, device, sends=None, takes=None):
+    def remote(src, dst, device, sends=None, takes=None, held=None):
         k = at[0]
         at[0] += 1
         copy = pltpu.make_async_remote_copy(
@@ -375,7 +384,10 @@
         if sends is None:
             copy.start()
             return copy.wait
-        pl.when(sends)(copy.start)
+        if held is None:
+            pl.when(sends)(copy.start)
+        else:
+            held.append((sends, copy))
 
         def wait():
             pl.when(sends)(copy.wait_send)
@@ -386,14 +398,23 @@
     step1 = []
     for d in range(1, ny):
         step1.append(remote(send1.at[lax.rem(my + d, ny)], recv1.at[d - 1], along_y[d - 1]))
+    pl.when(late)(ahead)
+    pl.when(me > 0)(middle)
+    pl.when(jnp.logical_and(me > 0, early))(product)
+    held = []
     leaf = [
-        remote(pos.at[:, count - halo : count], pos_low, after, has_high, has_low),
-        remote(charge.at[:, count - halo : count], charge_low, after, has_high, has_low),
-        remote(pos.at[:, 0:halo], pos_high, before, has_low, has_high),
-        remote(charge.at[:, 0:halo], charge_high, before, has_low, has_high),
+        remote(pos.at[:, count - halo : count], pos_low, after, has_high, has_low, held),
+        remote(charge.at[:, count - halo : count], charge_low, after, has_high, has_low, held),
+        remote(pos.at[:, 0:halo], pos_high, before, has_low, has_high, held),
+        remote(charge.at[:, 0:halo], charge_high, before, has_low, has_high, held),
     ]
-    pl.when(jnp.logical_not(early))(ahead)
-    pl.when(me > 0)(middle)
+    rims = [
+        remote(last, low, after, has_high, has_low, held),
+        remote(first, high, before, has_low, has_high, held),
+    ]
+    soon = [early] * len(leaf) + [me < ny] * len(rims)
+    for (sends, copy), first_turn in zip(held, soon):
+        pl.when(jnp.logical_and(sends, first_turn))(copy.start)
     half = jnp.where(me < 2, quads, jnp.where(early, jnp.minimum(2, quads), 1))
     lax.fori_loop(1, half, step, 0)
 
@@ -414,15 +435,11 @@
         if d > 0:
             step2.append(remote(send2.at[row], recv2.at[d - 1], along_x[d - 1]))
 
-    rims = [
-        remote(last, low, after, has_high, has_low),
-        remote(first, high, before, has_low, has_high),
-    ]
+    for (sends, copy), first_turn in zip(held, soon):
+        pl.when(jnp.logical_and(sends, jnp.logical_not(first_turn)))(copy.start)
+    pl.when(late)(product)
 
     lax.fori_loop(half, quads, step, 0)
-
-    lanes = spread.shape[0]
-    alive = alive_lanes(live[...], slots, (surface, lanes))
 
     for wait in leaf:
         wait()
@@ -440,23 +457,29 @@
 
     for wait in rims:
         wait()
-    window[:, 0:rim] = jnp.where(has_low, low[...], jnp.zeros_like(low))
+    spread[...] = jnp.zeros_like(spread)
+    spread[0:rim, :] = jnp.where(has_low, low[...].astype(f32), f32(0.0))
+    top = lanes - rim
+    spread[top:, :] = jnp.where(has_high, high[...].astype(f32), f32(0.0))
+    slot = row_ids((own, surface)) // Q
+    lower = live[...] // 2
+    alive = (slot < lower) | (slot >= slots - (live[...] - lower))
     for wait in step2:
         wait()
     shared = send2[mx]
     for d in range(nx - 1):
         shared = shared + recv2[d]
-    spread[...] = jnp.zeros_like(spread)
-    spread[0:own, :] = shared
-    front = local[:, 0:lanes].astype(f32) + spread[...].T
-    front = jnp.where(alive, front, f32(0.0)).astype(bf16)
-    window[:, rim : rim + lanes] = front
+    spread[rim : rim + own, :] = jnp.where(alive, shared, f32(0.0))
     shared = recv3[0]
     for d in range(1, nx):
         shared = shared + recv3[d]
-    spread[0:own, :] = shared
-    front = high[...].astype(f32) + spread[...].T[:, 0:rim]
-    window[:, rim + wide :] = jnp.where(has_high, front, f32(0.0)).astype(bf16)
+    shared = spread[top : top + own, :] + shared
+    spread[top : top + own, :] = jnp.where(has_high, shared, f32(0.0))
+    turned = spread[...].T
+    front = lane_ids(turned.shape) < top
+    front = window[:, 0:lanes].astype(f32) + jnp.where(front, turned, f32(0.0))
+    window[:, 0:lanes] = front.astype(bf16)
+    window[:, rim + wide :] = turned[:, top:].astype(bf16)
 
 
 def fused(live, child, users, local, pos, charge, nbrs, lists, ops):
@@ -497,10 +520,10 @@
             pltpu.VMEM((nx - 1, own, surface), f32),
             pltpu.VMEM((nx, own, surface), f32),
             pltpu.VMEM((128, surface), f32),
-            pltpu.VMEM((surface, rim), bf16),
-            pltpu.VMEM((surface, rim), bf16),
-            pltpu.VMEM((surface, rim), bf16),
-            pltpu.VMEM((surface, rim), bf16),
+            pltpu.VMEM((rim, surface), bf16),
+            pltpu.VMEM((rim, surface), bf16),
+            pltpu.VMEM((rim, surface), bf16),
+            pltpu.VMEM((rim, surface), bf16),
             pltpu.VMEM((3, halo), f32),
             pltpu.VMEM((3, halo), f32),
             pltpu.VMEM((Q, halo), f32),

time: 17.9 us -> 17.4 us (0.972)
  the two profiles are of different devices: /device:TPU:0 before, /device:TPU:17 now
where the time goes in v3:
time: 17.4 us; the launch traced here: 17.2 us
  Pallas kernels  15.8 us (91%)
  between operations  1.45 us (8%)
    pallas_call x1, Pallas kernels, fused(): pl.pallas_call(functools.partial(fused_kernel, nx, ny), out_shape=(jax.Sh...  13.6 us
    pallas_call x1, Pallas kernels, m2l(): pl.pallas_call(m2l_kernel, out_shape=(jax.ShapeDtypeStruct((surface, wide...  2.15 us

profile of v3, /device:TPU:17, one launch (start us, length us, event | category | flops | bytes accessed | tf_op | source)
XLA Modules:
  0.0 17.2 jit_solution(13609210030899458730)
XLA Ops:
  1.3 13.6 %shard_map.104 = (bf16[296,576]{1,0:T(8,128)(2,1)S(1)}, f32[4,4096]{1,0:T(4,128)S(1)}, f32[296,256]{1,0:T(8,128)S(1)}, s32[8,128]{1,0:T(8,128)S(1)}, bf16[296,2368]{1,0:T(8,128)(2,1)S(1)}) custom-call(s32[1,1]{1,0:T(1,128)} %bitcast.3.live_in, bf16[296,256]{1,0:T(8,128)(2,1)} %child_in.1, s32[1,64]{1,0:T(1,128)} %bitcast.6, bf16[296,512]{1,0:T(8,128)(2,1)} %local_in.1, ...), custom_call_target="tpu_custom_call" | custom-call | tf_op jit(solution)/shard_map/pallas_call | solution.py:503
  14.9 2.1 %shard_map.105 = (f32[296,512]{1,0:T(8,128)}, f32[4,4096]{1,0:T(4,128)}) custom-call(s32[1,1]{1,0:T(1,128)} %bitcast.4.live, bf16[296,576]{1,0:T(8,128)(2,1)S(1)} %get-tuple-element.7.window, s32[8,128]{1,0:T(8,128)S(1)} %get-tuple-element.8.lists, bf16[296,2368]{1,0:T(8,128)(2,1)S(1)} %get-tuple-element.9.ops, f32[4,4096]{1,0:T(4,128)S(1)} %get-tuple-element.10.near, ...), custom_call_target="tpu_custom_call" | custom-call | tf_op jit(solution)/shard_map/pallas_call | solution.py:576

commit v4 on v3

--- a/solution.py
+++ b/solution.py
@@ -335,6 +335,7 @@
 
     early = me < 2 * ny
     late = me >= 2 * ny
+    final = me >= jnp.maximum(2, nx - 1) * ny
 
     def ahead():
         prepare()
@@ -365,6 +366,7 @@
     pl.when(early)(ahead)
     pl.when(me == 0)(middle)
     pl.when(me == 0)(product)
+    pl.when(jnp.logical_and(late, jnp.logical_not(final)))(prepare)
     neighbours = jnp.where(has_low, 1, 0) + jnp.where(has_high, 1, 0)
     pl.semaphore_wait(barrier, len(along_y) + len(along_x) + neighbours)
 
@@ -398,9 +400,10 @@
     step1 = []
     for d in range(1, ny):
         step1.append(remote(send1.at[lax.rem(my + d, ny)], recv1.at[d - 1], along_y[d - 1]))
-    pl.when(late)(ahead)
+    pl.when(final)(prepare)
+    lax.fori_loop(0, jnp.where(late, 1, 0), step, 0)
     pl.when(me > 0)(middle)
-    pl.when(jnp.logical_and(me > 0, early))(product)
+    pl.when(me > 0)(product)
     held = []
     leaf = [
         remote(pos.at[:, count - halo : count], pos_low, after, has_high, has_low, held),
@@ -437,7 +440,6 @@
 
     for (sends, copy), first_turn in zip(held, soon):
         pl.when(jnp.logical_and(sends, jnp.logical_not(first_turn)))(copy.start)
-    pl.when(late)(product)
 
     lax.fori_loop(half, quads, step, 0)
 

time: 17.4 us -> 17.9 us (1.029)
  the two profiles are of different devices: /device:TPU:17 before, /device:TPU:0 now
where the time goes in v4:
time: 17.9 us; the launch traced here: 17.8 us
  Pallas kernels  16.3 us (91%)
  between operations  1.45 us (8%)
    pallas_call x1, Pallas kernels, fused(): pl.pallas_call(functools.partial(fused_kernel, nx, ny), out_shape=(jax.Sh...  14.2 us
    pallas_call x1, Pallas kernels, m2l(): pl.pallas_call(m2l_kernel, out_shape=(jax.ShapeDtypeStruct((surface, wide...  2.15 us

profile of v4, /device:TPU:0, one launch (start us, length us, event | category | flops | bytes accessed | tf_op | source)
XLA Modules:
  0.0 17.8 jit_solution(17284059834413967090)
XLA Ops:
  1.3 14.2 %shard_map.104 = (bf16[296,576]{1,0:T(8,128)(2,1)S(1)}, f32[4,4096]{1,0:T(4,128)S(1)}, f32[296,256]{1,0:T(8,128)S(1)}, s32[8,128]{1,0:T(8,128)S(1)}, bf16[296,2368]{1,0:T(8,128)(2,1)S(1)}) custom-call(s32[1,1]{1,0:T(1,128)} %bitcast.3.live_in, bf16[296,256]{1,0:T(8,128)(2,1)} %child_in.1, s32[1,64]{1,0:T(1,128)} %bitcast.6, bf16[296,512]{1,0:T(8,128)(2,1)} %local_in.1, ...), custom_call_target="tpu_custom_call" | custom-call | tf_op jit(solution)/shard_map/pallas_call | solution.py:505
  15.5 2.1 %shard_map.105 = (f32[296,512]{1,0:T(8,128)}, f32[4,4096]{1,0:T(4,128)}) custom-call(s32[1,1]{1,0:T(1,128)} %bitcast.4.live, bf16[296,576]{1,0:T(8,128)(2,1)S(1)} %get-tuple-element.7.window, s32[8,128]{1,0:T(8,128)S(1)} %get-tuple-element.8.lists, bf16[296,2368]{1,0:T(8,128)(2,1)S(1)} %get-tuple-element.9.ops, f32[4,4096]{1,0:T(4,128)S(1)} %get-tuple-element.10.near, ...), custom_call_target="tpu_custom_call" | custom-call | tf_op jit(solution)/shard_map/pallas_call | solution.py:578
